TPU v7x, 32 devices: a whole 2x2x4 slice. The times are simulated.
32 devices in a mesh: seq: 4 (over y, core), tp: 8 (over z, x).
Axes of the slice: x: 2, y: 2, z: 4, core: 2. Of those that a mesh axis runs over, the one named last changes fastest.
Arguments:
- tokens: bfloat16 [2048, 8192], P('seq', 'tp'), may hold values from -6 to 6
- w_query: bfloat16 [8192, 6144], P(None, 'tp'), may hold values from -0.0625 to 0.0625
- w_key: bfloat16 [8192, 6144], P(None, 'tp'), may hold values from -0.0625 to 0.0625
- w_value: bfloat16 [8192, 6144], P(None, 'tp'), may hold values from -0.0625 to 0.0625
- w_out: bfloat16 [6144, 8192], P('tp'), may hold values from -0.109375 to 0.109375
- carry: float32 [48, 128, 128], P('tp'), may hold values from -40 to 40
Outputs:
- mixed: bfloat16 [2048, 8192], P('seq', 'tp')
All inputs are finite; a program needn't handle non-finite values.
Results may differ from a plain program's by a relative error of at most 0.0066.
Values may be sent and summed in bfloat16 or wider, within the bound.
No kernel may reach another device: no remote copies, remote signals or barrier semaphores. Data moves between devices by JAX's collectives and lax.ppermute only.
A program may use at most 192 MiB of HBM per device.

v0:
```python
import jax
import jax.numpy as jnp
from jax import lax
from jax.sharding import PartitionSpec as P

EPSILON = 1e-05


def entering(array, axis, combine, identity):
    count, place = (lax.axis_size(axis), lax.axis_index(axis))
    everything = lax.all_gather(array, axis)
    start = jnp.broadcast_to(jnp.asarray(identity, array.dtype), array.shape)

    def turn(k, before):
        reached = k < place
        new = combine(before, everything[k])
        return jnp.where(reached, new, before)

    return lax.fori_loop(0, count, turn, start)


def combine_states(earlier, latter_part):
    return earlier + latter_part


def local(tokens, w_query, w_key, w_value, w_out, carry):
    row_count = tokens.shape[0]
    head_count = carry.shape[0]
    head_size = carry.shape[1]
    proj_width = w_query.shape[1]
    segment = lax.all_gather(tokens, "tp", axis=1, tiled=True)
    query_sum = jnp.dot(segment, w_query, preferred_element_type=jnp.float32)
    key_sum = jnp.dot(segment, w_key, preferred_element_type=jnp.float32)
    value_sum = jnp.dot(segment, w_value, preferred_element_type=jnp.float32)
    query = query_sum.astype(jnp.bfloat16).reshape(row_count, head_count, head_size)
    keys_local = key_sum.astype(jnp.bfloat16).reshape(row_count, head_count, head_size)
    values_local = value_sum.astype(jnp.bfloat16).reshape(row_count, head_count, head_size)
    local_state = jnp.einsum(
        "thd,the->hde", keys_local, values_local, preferred_element_type=jnp.float32
    )
    earlier_sum = entering(local_state, "seq", combine_states, jnp.zeros_like(local_state))
    prior = carry + earlier_sum
    across = jnp.einsum(
        "thd,hde->the", query.astype(jnp.float32), prior, precision=lax.Precision.HIGHEST
    )
    causal = lax.broadcasted_iota(jnp.int32, (row_count, row_count), 0) >= lax.broadcasted_iota(
        jnp.int32, (row_count, row_count), 1
    )
    scores = jnp.einsum("thd,shd->hts", query, keys_local, preferred_element_type=jnp.float32)
    scores = jnp.where(causal[None], scores, 0.0).astype(jnp.bfloat16)
    within = jnp.einsum("hts,she->the", scores, values_local, preferred_element_type=jnp.float32)
    total = across + within
    normed = total * lax.rsqrt(jnp.mean(total * total, axis=-1, keepdims=True) + EPSILON)
    attended = normed.astype(jnp.bfloat16).reshape(row_count, proj_width)
    summed = lax.psum_scatter(
        lax.dot_general(
            w_out, attended, (((0,), (1,)), ((), ())), preferred_element_type=jnp.float32
        ),
        "tp",
        scatter_dimension=0,
        tiled=True,
    )
    return summed.T.astype(jnp.bfloat16)


def solution(mesh):
    placed = (
        P("seq", "tp"),
        P(None, "tp"),
        P(None, "tp"),
        P(None, "tp"),
        P("tp", None),
        P("tp", None, None),
    )
    return jax.shard_map(
        local, mesh=mesh, in_specs=placed, out_specs=P("seq", "tp"), check_vma=False
    )
```

profile of v0, /device:TPU:0, one launch (start us, length us, event | category | flops | bytes accessed | tf_op | source)
XLA Modules:
  0.0 496.5 jit_solution(3666014107982523729)
XLA Ops:
  6.5 0.0 all-gather.4.cloned.1.call-start
  6.5 0.7 all-gather.4.cloned.1.call-update
  7.3 0.0 all-gather.6.cloned.1.call-start
  7.3 129.9 %all-gather.4.cloned.1.call-done = bf16[512,8192]{1,0:T(8,128)(2,1)} async-done(((bf16[512,1024]{1,0:T(8,128)(2,1)}), bf16[512,8192]{1,0:T(8,128)(2,1)}) %all-gather.4.cloned.1.call-update) | async-done | bytes 8388624 | tf_op jit(solution)/shard_map/all_gather | solution.py:31
  137.2 12.7 %convolution_convert_fusion.2 = bf16[512,768]{1,0:T(8,128)(2,1)S(1)} fusion(bf16[512,8192]{1,0:T(8,128)(2,1)} %all-gather.4.cloned.1.call-done, bf16[8192,768]{1,0:T(8,128)(2,1)} %param.10), kind=kOutput, calls=%fused_computation.14 | convolution fusion | flops 6442844160 | bytes 21757952 | tf_op jit(solution)/shard_map/dot_general | solution.py:33
  149.9 0.3 copy.18
  150.2 12.7 %convolution_convert_fusion.1 = bf16[512,768]{1,0:T(8,128)(2,1)S(1)} fusion(bf16[512,8192]{1,0:T(8,128)(2,1)} %all-gather.4.cloned.1.call-done, bf16[8192,768]{1,0:T(8,128)(2,1)} %param.11), kind=kOutput, calls=%fused_computation.13 | convolution fusion | flops 6442844160 | bytes 21757952 | tf_op jit(solution)/shard_map/dot_general | solution.py:34
  162.9 0.3 copy.19
  163.2 1.1 fusion.9
  164.3 0.0 all-gather.6.cloned.1.call-update
  164.3 0.2 reduce-scatter.2.cloned.1.call-start
  164.6 0.8 iota_compare_fusion
  165.3 13.2 %convolution_convert_fusion = bf16[512,768]{1,0:T(8,128)(2,1)S(1)} fusion(bf16[512,8192]{1,0:T(8,128)(2,1)} %all-gather.4.cloned.1.call-done, bf16[8192,768]{1,0:T(8,128)(2,1)} %param.9), kind=kOutput, calls=%fused_computation.12 | convolution fusion | flops 6442844160 | bytes 21757952 | tf_op jit(solution)/shard_map/dot_general | solution.py:32
  178.6 0.3 copy.21
  178.9 0.0 copy-start
  178.9 4.2 fusion
  183.1 0.0 all-gather.6.cloned.1.call-done
  183.1 4.6 while.14
  183.1 1.1 add_select_fusion.2
  184.2 1.1 add_select_fusion.2
  185.4 1.1 add_select_fusion.2
  186.5 1.1 add_select_fusion.2
  187.7 0.0 copy-done
  187.7 2.4 fusion.5
  190.1 0.2 fusion.6
  190.3 14.8 %convolution_bitcast_fusion = f32[8192,512]{0,1:T(8,128)} fusion(bf16[512,768]{0,1:T(8,128)(2,1)S(1)} %bitcast.34, bf16[768,8192]{1,0:T(8,128)(2,1)} %param.12), kind=kOutput, calls=%fused_computation.1 | convolution fusion | flops 6442450944 | bytes 30146560 | tf_op jit(solution)/shard_map/dot_general | solution.py:56
  205.1 0.0 reduce-scatter.2.cloned.1.call-update
  205.1 282.1 %reduce-scatter.2.cloned.1.call-done = f32[1024,512]{0,1:T(8,128)} async-done(((f32[8192,512]{0,1:T(8,128)}), f32[1024,512]{0,1:T(8,128)}) %reduce-scatter.2.cloned.1.call-update) | async-done | bytes 2097168 | tf_op jit(solution)/shard_map/reduce_scatter | solution.py:55
  487.2 2.7 convert_bitcast_fusion
  (2 shorter events, 0.0 us)
Async XLA Ops:
  6.5 130.7 %all-gather.4.cloned.1.call-start = ((), (), s32[]{:S(2)}) async-start(), calls=%async_computation.1 | async-start | bytes 9437184 | tf_op jit(solution)/shard_map/all_gather | solution.py:31
  7.3 175.8 %all-gather.6.cloned.1.call-start = ((), (), s32[]{:S(2)}) async-start(), calls=%async_computation.3 | async-start | bytes 1966080 | tf_op jit(solution)/shard_map/all_gather | solution.py:11
  164.3 322.9 %reduce-scatter.2.cloned.1.call-start = ((), (), s32[]{:S(2)}) async-start(), calls=%async_computation.2 | async-start | bytes 18874368 | tf_op jit(solution)/shard_map/reduce_scatter | solution.py:55
  178.9 8.8 %copy-start = (f32[6,128,128]{2,1,0:T(8,128)S(1)}, f32[6,128,128]{2,1,0:T(8,128)}, u32[]{:S(2)}) copy-start(f32[6,128,128]{2,1,0:T(8,128)} %param.13) | copy-start | bytes 1179652
Sparse Core Ops, SparseCore 0:
  9.5 127.5 all-gather.3
  164.4 17.8 all-gather.5
  205.2 281.9 reduce-scatter.1
where the time goes:
time: 497 us; the launch traced here: 496 us
  waiting for transfers between devices  413 us (83%)
  matrix products  61.1 us (12%)
  between operations  13.2 us (3%)
  other arithmetic  8.24 us (2%)
    reduce_scatter x1, waiting for transfers between devices, local(): lax.psum_scatter(lax.dot_general(w_out, attended, (((0,), (1,)), ((), ())...  282 us
    all_gather x1, waiting for transfers between devices, local(): segment = lax.all_gather(tokens, 'tp', axis=1, tiled=True)  130 us
    dot_general x1, matrix products, local(): lax.dot_general(w_out, attended, (((0,), (1,)), ((), ())), preferred_elem...  14.8 us
    dot_general x1, matrix products, local(): query_sum = jnp.dot(segment, w_query, preferred_element_type=jnp.float32)  13.2 us
    dot_general x1, matrix products, local(): key_sum = jnp.dot(segment, w_key, preferred_element_type=jnp.float32)  12.7 us
    dot_general x1, matrix products, local(): value_sum = jnp.dot(segment, w_value, preferred_element_type=jnp.float32)  12.7 us
  transfers between devices with their start and end apart: 3, of which 2 were waited for; matrix products, arithmetic and copies ran while one was open for 4% of the time, Pallas kernels for 0%

commit v1 on v0

--- a/solution.py
+++ b/solution.py
@@ -4,6 +4,24 @@
 from jax.sharding import PartitionSpec as P
 
 EPSILON = 1e-05
+
+
+def joined_along(blocks, dim):
+    shape = list(blocks.shape[1:])
+    shape[dim] *= blocks.shape[0]
+    return jnp.moveaxis(blocks, 0, dim).reshape(shape)
+
+
+def doubled(value, axis):
+    size = lax.axis_size(axis)
+    blocks = value[None]
+    for level in range(size.bit_length() - 1):
+        stride = 1 << level
+        other = lax.ppermute(blocks, axis, [(i, i ^ stride) for i in range(size)])
+        both = jnp.stack([blocks, other])
+        upper = lax.axis_index(axis) >> level & 1
+        blocks = jnp.where(upper == 0, both, both[::-1]).reshape(-1, *value.shape)
+    return blocks
 
 
 def entering(array, axis, combine, identity):
@@ -28,7 +46,7 @@
     head_count = carry.shape[0]
     head_size = carry.shape[1]
     proj_width = w_query.shape[1]
-    segment = lax.all_gather(tokens, "tp", axis=1, tiled=True)
+    segment = joined_along(doubled(tokens, "tp"), 1)
     query_sum = jnp.dot(segment, w_query, preferred_element_type=jnp.float32)
     key_sum = jnp.dot(segment, w_key, preferred_element_type=jnp.float32)
     value_sum = jnp.dot(segment, w_value, preferred_element_type=jnp.float32)

time: 497 us -> 656 us (1.32)
  waiting for transfers between devices: 413 us -> 527 us
  other arithmetic: 8.24 us -> 36 us
  local copies, waits for them, and re-layouts: 0.84 us -> 13.3 us
  starting transfers between devices: 0.26 us -> 7.33 us
    ppermute x0 -> x3, waiting for transfers between devices: none -> 242 us  [doubled(): other = lax.ppermute(blocks, axis, [(i, i ^ stride) for i in range(size)])]
    all_gather x1 -> x0, waiting for transfers between devices: 130 us -> none  [local(): segment = lax.all_gather(tokens, 'tp', axis=1, tiled=True)]
    select_n x0 -> x2, other arithmetic: none -> 14.7 us  [doubled(): blocks = jnp.where(upper == 0, both, both[::-1]).reshape(-1, *value.shape)]
    another operation x0 -> x4, other arithmetic: none -> 13 us  [doubled(): both = jnp.stack([blocks, other])]
    ppermute x0 -> x3, starting transfers between devices: none -> 7.29 us  [doubled(): other = lax.ppermute(blocks, axis, [(i, i ^ stride) for i in range(size)])]
  transfers between devices with their start and end apart: 3 -> 5, of which waited for: 2 -> 5; matrix products, arithmetic and copies ran while one was open for 4% -> 4% of each run, Pallas kernels for 0% -> 0%
where the time goes in v1:
time: 656 us; the launch traced here: 655 us
  waiting for transfers between devices  527 us (80%)
  matrix products  58 us (9%)
  other arithmetic  36 us (5%)
  between operations  13.5 us (2%)
  local copies, waits for them, and re-layouts  13.3 us (2%)
  starting transfers between devices  7.33 us (1%)
    reduce_scatter x1, waiting for transfers between devices, local(): lax.psum_scatter(lax.dot_general(w_out, attended, (((0,), (1,)), ((), ())...  283 us
    ppermute x3, waiting for transfers between devices, doubled(): other = lax.ppermute(blocks, axis, [(i, i ^ stride) for i in range(size)])  242 us
    dot_general x1, matrix products, local(): lax.dot_general(w_out, attended, (((0,), (1,)), ((), ())), preferred_elem...  14.8 us
    select_n x2, other arithmetic, doubled(): blocks = jnp.where(upper == 0, both, both[::-1]).reshape(-1, *value.shape)  14.7 us
  transfers between devices with their start and end apart: 5, of which 5 were waited for; matrix products, arithmetic and copies ran while one was open for 4% of the time, Pallas kernels for 0%

profile of v1, /device:TPU:0, one launch (start us, length us, event | category | flops | bytes accessed | tf_op | source)
XLA Modules:
  0.0 655.5 jit_solution(2264821831291554191)
XLA Ops:
  6.5 2.9 collective-permute-start
  9.5 23.4 %collective-permute-done = bf16[1,512,1024]{2,1,0:T(8,128)(2,1)S(1)} collective-permute-done((bf16[1,512,1024]{2,1,0:T(8,128)(2,1)}, bf16[1,512,1024]{2,1,0:T(8,128)(2,1)S(1)}, u32[]{:S(2)}, u32[]{:S(2)}) %collective-permute-start) | collective-permute-done | bytes 1048608 | tf_op jit(solution)/shard_map/ppermute | solution.py:20
  32.8 1.4 pad_maximum_fusion.2
  34.3 2.2 fusion.6
  36.4 1.8 collective-permute-start.1
  38.3 45.3 %collective-permute-done.1 = bf16[2,512,1024]{2,1,0:T(8,128)(2,1)} collective-permute-done((bf16[2,512,1024]{2,1,0:T(8,128)(2,1)}, bf16[2,512,1024]{2,1,0:T(8,128)(2,1)}, u32[]{:S(2)}, u32[]{:S(2)}) %collective-permute-start.1) | collective-permute-done | bytes 2097184 | tf_op jit(solution)/shard_map/ppermute | solution.py:20
  83.6 2.0 pad_maximum_fusion.1
  85.6 3.2 reverse_select_fusion.1
  88.7 6.2 copy.20
  95.0 2.5 collective-permute-start.2
  97.5 6.3 copy.21
  103.8 173.2 %collective-permute-done.2 = bf16[4,512,1024]{1,2,0:T(8,128)(2,1)} collective-permute-done((bf16[4,512,1024]{1,2,0:T(8,128)(2,1)}, bf16[4,512,1024]{1,2,0:T(8,128)(2,1)}, u32[]{:S(2)}, u32[]{:S(2)}) %collective-permute-start.2) | collective-permute-done | bytes 4194336 | tf_op jit(solution)/shard_map/ppermute | solution.py:20
  276.9 7.5 %pad_maximum_fusion = bf16[2,4,512,1024]{2,3,1,0:T(8,128)(2,1)} fusion(bf16[1,4,512,1024]{2,3,1,0:T(8,128)(2,1)} %bitcast.8, bf16[1,4,512,1024]{2,3,1,0:T(8,128)(2,1)} %copy.21), kind=kLoop, calls=%fused_computation.3 | loop fusion | flops 4194304 | bytes 16777216 | tf_op jit(solution)/shard_map/stack | solution.py:21
  284.4 11.5 %reverse_select_fusion = bf16[2,4,512,1024]{2,3,1,0:T(8,128)(2,1)} fusion(bf16[2,4,512,1024]{2,3,1,0:T(8,128)(2,1)} %pad_maximum_fusion, pred[]{:T(512)S(6)} %eq.9), kind=kLoop, calls=%fused_computation.2 | loop fusion | flops 4194304 | bytes 16777216 | tf_op jit(solution)/shard_map/jit(_where)/select_n | solution.py:23
  295.9 12.9 %convolution_convert_fusion.1 = bf16[512,768]{1,0:T(8,128)(2,1)S(1)} fusion(bf16[512,8192]{0,1:T(8,128)(2,1)} %bitcast.52, bf16[8192,768]{1,0:T(8,128)(2,1)} %param.11), kind=kOutput, calls=%fused_computation.21 | convolution fusion | flops 6442844160 | bytes 21757952 | tf_op jit(solution)/shard_map/dot_general | solution.py:52
  308.8 9.9 %convolution_convert_fusion.2 = bf16[512,768]{1,0:T(8,128)(2,1)S(1)} fusion(bf16[512,8192]{0,1:T(8,128)(2,1)S(1)} %bitcast.54, bf16[8192,768]{1,0:T(8,128)(2,1)} %param.10), kind=kOutput, calls=%fused_computation.22 | convolution fusion | flops 6442844160 | bytes 21757952 | tf_op jit(solution)/shard_map/dot_general | solution.py:51
  318.8 0.3 copy.22
  319.1 0.3 copy.23
  319.3 1.1 fusion.11
  320.5 0.8 iota_compare_fusion
  321.3 12.8 %convolution_convert_fusion = bf16[512,768]{1,0:T(8,128)(2,1)S(1)} fusion(bf16[512,8192]{0,1:T(8,128)(2,1)} %bitcast.53, bf16[8192,768]{1,0:T(8,128)(2,1)} %param.9), kind=kOutput, calls=%fused_computation.20 | convolution fusion | flops 6442844160 | bytes 21757952 | tf_op jit(solution)/shard_map/dot_general | solution.py:50
  334.4 4.1 fusion
  338.5 2.6 all-gather.3.cloned.1.call-done
  341.0 4.6 while.14
  341.0 1.1 add_select_fusion.2
  342.2 1.1 add_select_fusion.2
  343.4 1.1 add_select_fusion.2
  344.5 1.1 add_select_fusion.2
  345.7 2.4 fusion.7
  348.3 14.8 %convolution_bitcast_fusion = f32[8192,512]{0,1:T(8,128)} fusion(bf16[512,768]{0,1:T(8,128)(2,1)S(1)} %bitcast.55, bf16[768,8192]{1,0:T(8,128)(2,1)} %param.12), kind=kOutput, calls=%fused_computation.1 | convolution fusion | flops 6442450944 | bytes 30146560 | tf_op jit(solution)/shard_map/dot_general | solution.py:74
  363.1 282.8 %reduce-scatter.2.cloned.1.call-done = f32[1024,512]{0,1:T(8,128)} async-done(((f32[8192,512]{0,1:T(8,128)}), f32[1024,512]{0,1:T(8,128)}) %reduce-scatter.2.cloned.1.call-update) | async-done | bytes 2097168 | tf_op jit(solution)/shard_map/reduce_scatter | solution.py:73
  645.9 2.7 convert_bitcast_fusion
  (12 shorter events, 0.6 us)
Async XLA Ops:
  6.5 334.5 %all-gather.3.cloned.1.call-start = ((), (), s32[]{:S(2)}) async-start(), calls=%async_computation.2 | async-start | bytes 1966080 | tf_op jit(solution)/shard_map/all_gather | solution.py:29
  6.5 26.3 %collective-permute-start = (bf16[1,512,1024]{2,1,0:T(8,128)(2,1)}, bf16[1,512,1024]{2,1,0:T(8,128)(2,1)S(1)}, u32[]{:S(2)}, u32[]{:S(2)}) collective-permute-start(bf16[1,512,1024]{2,1,0:T(8,128)(2,1)} %bitcast.63), channel_id=1, source_target_pairs={{0,1},{1,0},{2,3},{3,2},{4,5},{5,4},{6,7},{7,6},{8,9},{9,8},{10,11... | collective-permute-start | bytes 3145736 | tf_op jit(solution)/shard_map/ppermute | solution.py:20
  36.4 47.1 %collective-permute-start.1 = (bf16[2,512,1024]{2,1,0:T(8,128)(2,1)}, bf16[2,512,1024]{2,1,0:T(8,128)(2,1)}, u32[]{:S(2)}, u32[]{:S(2)}) collective-permute-start(bf16[2,512,1024]{2,1,0:T(8,128)(2,1)} %get-tuple-element.109), channel_id=1, source_target_pairs={{0,2},{1,3},{2,0},{3,1},{4,6},{5,7},{6,4},{7,5},{8,10},{9,11},{10,... | collective-permute-start | bytes 6291464 | tf_op jit(solution)/shard_map/ppermute | solution.py:20
  95.0 181.9 %collective-permute-start.2 = (bf16[4,512,1024]{1,2,0:T(8,128)(2,1)}, bf16[4,512,1024]{1,2,0:T(8,128)(2,1)}, u32[]{:S(2)}, u32[]{:S(2)}) collective-permute-start(bf16[4,512,1024]{1,2,0:T(8,128)(2,1)} %copy.20), channel_id=1, source_target_pairs={{0,4},{1,5},{2,6},{3,7},{4,0},{5,1},{6,2},{7,3},{8,12},{9,13},{10,... | collective-permute-start | bytes 12582920 | tf_op jit(solution)/shard_map/ppermute | solution.py:20
  295.9 12.9 %copy-start = (bf16[2,4,512,1024]{2,3,1,0:T(8,128)(2,1)S(1)}, bf16[2,4,512,1024]{2,3,1,0:T(8,128)(2,1)}, u32[]{:S(2)}) copy-start(bf16[2,4,512,1024]{2,3,1,0:T(8,128)(2,1)} %reverse_select_fusion) | copy-start | bytes 25165828
  320.5 325.4 %reduce-scatter.2.cloned.1.call-start = ((), (), s32[]{:S(2)}) async-start(), calls=%async_computation.1 | async-start | bytes 18874368 | tf_op jit(solution)/shard_map/reduce_scatter | solution.py:73
  338.5 7.2 %copy-start.1 = (f32[6,128,128]{2,1,0:T(8,128)S(1)}, f32[6,128,128]{2,1,0:T(8,128)}, u32[]{:S(2)}) copy-start(f32[6,128,128]{2,1,0:T(8,128)} %param.13) | copy-start | bytes 1179652
Sparse Core Ops, SparseCore 0:
  320.6 20.4 all-gather.2
  363.2 282.6 reduce-scatter.1
